TPU v7x, 256 devices: a whole 4x4x8 slice. The times are simulated.
256 devices in a mesh: dp: 8 (over z), expert: 32 (over x, y, core).
Axes of the slice: x: 4, y: 4, z: 8, core: 2. Of those that a mesh axis runs over, the one named last changes fastest.
Arguments:
- tokens: bfloat16 [32768, 2048], P(('dp', 'expert')), may hold values from -24 to 24
- expert_ids: int32 [32768, 2], P(('dp', 'expert')), may hold values from 0 to 31, all different within a row; in each aligned block of 128 rows (0 to 127, 128 to 255, ...) at most 16 rows name the same one
- gate_probs: float32 [32768, 2], P(('dp', 'expert')), may hold values from 0.1 to 1
- w_gate: bfloat16 [32, 2048, 768], P('expert'), may hold values from -0.125 to 0.125
- w_up: bfloat16 [32, 2048, 768], P('expert'), may hold values from -0.125 to 0.125
- w_down: bfloat16 [32, 2048, 768], P('expert'), may hold values from -0.21875 to 0.21875
- out_grad: bfloat16 [32768, 2048], P(('dp', 'expert')), may hold values from -6 to 6
Outputs:
- mixed: bfloat16 [32768, 2048], P(('dp', 'expert'))
- tokens_grad: bfloat16 [32768, 2048], P(('dp', 'expert'))
- grad_gate: bfloat16 [32, 2048, 768], P('expert', 'dp')
- grad_up: bfloat16 [32, 2048, 768], P('expert', 'dp')
- grad_down: bfloat16 [32, 2048, 768], P('expert', 'dp')
Inputs may be any that keep to these rules, and one draw needn't show every extreme that they name: `expert_ids`: within each group of 128 tokens no expert is chosen by more than 16 tokens, and some expert reaches 16; a token's 2 experts differ; every expert is chosen somewhere.
All inputs are finite; a program needn't handle non-finite values.
Results may differ from a plain program's by a relative error of at most 0.014.
Values may be sent and summed in bfloat16 or wider, within the bound.
A program may use at most 128 MiB of HBM per device.

v0:
```python
import jax
import jax.numpy as jnp
from jax import lax
from jax.sharding import PartitionSpec as P


def route_slots(expert_ids, experts, capacity):
    flat = expert_ids.reshape(-1)
    onehot = (flat[:, None] == jnp.arange(experts, dtype=jnp.int32)[None, :]).astype(jnp.int32)
    before = jnp.cumsum(onehot, axis=0) - onehot
    position = jnp.sum(before * onehot, axis=1)
    return flat * capacity + position


def local(tokens, expert_ids, gate_probs, w_gate, w_up, w_down, out_grad):
    token_count, top_count = expert_ids.shape
    width = tokens.shape[1]
    local_experts = w_gate.shape[0]
    peers = lax.axis_size("expert")
    experts = local_experts * peers
    capacity = max(2, 2 * token_count * top_count // experts)
    slot_total = experts * capacity
    route_total = token_count * top_count
    slot = route_slots(expert_ids, experts, capacity)
    owner = slot[None, :] == jnp.arange(slot_total, dtype=jnp.int32)[:, None]
    live = jnp.any(owner, axis=1)
    route_index = jnp.sum(
        jnp.where(owner, jnp.arange(route_total, dtype=jnp.int32)[None, :], 0), axis=1
    )
    token_of_slot = route_index // top_count
    slot_prob = jnp.sum(jnp.where(owner, gate_probs.reshape(-1)[None, :], 0.0), axis=1)
    dispatched = jnp.where(
        live[:, None], jnp.take(tokens, token_of_slot, axis=0), jnp.zeros((), tokens.dtype)
    )
    dispatched = dispatched.reshape(peers, local_experts, capacity, width)
    expert_received = lax.all_to_all(dispatched, "expert", split_axis=0, concat_axis=0, tiled=True)
    gate_act = jnp.einsum(
        "secd,edh->sech", expert_received, w_gate, preferred_element_type=jnp.float32
    )
    up_act = jnp.einsum("secd,edh->sech", expert_received, w_up, preferred_element_type=jnp.float32)
    expert_hidden = (jax.nn.silu(gate_act) * up_act).astype(jnp.bfloat16)
    result = jnp.einsum(
        "sech,edh->secd", expert_hidden, w_down, preferred_element_type=jnp.float32
    ).astype(jnp.bfloat16)
    returned = lax.all_to_all(result, "expert", split_axis=0, concat_axis=0, tiled=True)
    returned, gate_act, up_act, hidden, received = (
        returned,
        gate_act,
        up_act,
        expert_hidden,
        expert_received,
    )
    picked = jnp.take(returned.reshape(slot_total, width), slot, axis=0).astype(jnp.float32)
    picked = picked.reshape(token_count, top_count, width)
    mixed = jnp.sum(picked * gate_probs[:, :, None], axis=1).astype(jnp.bfloat16)
    dy_rows = jnp.where(
        live[:, None], jnp.take(out_grad, token_of_slot, axis=0), jnp.zeros((), out_grad.dtype)
    )
    dy_slot = (dy_rows.astype(jnp.float32) * slot_prob[:, None]).astype(jnp.bfloat16)
    dy_slot = dy_slot.reshape(peers, local_experts, capacity, width)
    dy_recv = lax.all_to_all(dy_slot, "expert", split_axis=0, concat_axis=0, tiled=True)
    d_hidden = jnp.einsum("secd,edh->sech", dy_recv, w_down, preferred_element_type=jnp.float32)
    sigma = jax.nn.sigmoid(gate_act)
    d_gate = (d_hidden * up_act * sigma * (1.0 + gate_act * (1.0 - sigma))).astype(jnp.bfloat16)
    d_up = (d_hidden * gate_act * sigma).astype(jnp.bfloat16)
    dx_slot = jnp.einsum("sech,edh->secd", d_gate, w_gate, preferred_element_type=jnp.float32)
    dx_slot = (
        dx_slot + jnp.einsum("sech,edh->secd", d_up, w_up, preferred_element_type=jnp.float32)
    ).astype(jnp.bfloat16)
    dx_back = lax.all_to_all(dx_slot, "expert", split_axis=0, concat_axis=0, tiled=True)
    dx_picked = jnp.take(dx_back.reshape(slot_total, width), slot, axis=0).astype(jnp.float32)
    tokens_grad = jnp.sum(dx_picked.reshape(token_count, top_count, width), axis=1).astype(
        jnp.bfloat16
    )
    columns = received
    first = jnp.einsum("secd,sech->deh", columns, d_gate, preferred_element_type=jnp.float32)
    second = jnp.einsum("secd,sech->deh", columns, d_up, preferred_element_type=jnp.float32)
    both = jnp.stack([first, second], axis=1)
    columns = dy_recv
    share = lax.psum_scatter(
        jnp.concatenate(
            [
                both,
                jnp.einsum("secd,sech->deh", columns, hidden, preferred_element_type=jnp.float32)[
                    :, None
                ],
            ],
            axis=1,
        ).astype(jnp.bfloat16),
        "dp",
        scatter_dimension=0,
        tiled=True,
    ).astype(jnp.float32)
    grad_gate = share[:, 0]
    grad_up = share[:, 1]
    grad_down = share[:, 2]
    grad_gate = jnp.transpose(grad_gate, (1, 0, 2)).astype(jnp.bfloat16)
    grad_up = jnp.transpose(grad_up, (1, 0, 2)).astype(jnp.bfloat16)
    grad_down = jnp.transpose(grad_down, (1, 0, 2)).astype(jnp.bfloat16)
    return (mixed, tokens_grad, grad_gate, grad_up, grad_down)


def solution(mesh):
    placed = (
        P(("dp", "expert"), None),
        P(("dp", "expert"), None),
        P(("dp", "expert"), None),
        P("expert", None, None),
        P("expert", None, None),
        P("expert", None, None),
        P(("dp", "expert"), None),
    )
    return jax.shard_map(
        local,
        mesh=mesh,
        in_specs=placed,
        out_specs=(
            P(("dp", "expert"), None),
            P(("dp", "expert"), None),
            P("expert", "dp", None),
            P("expert", "dp", None),
            P("expert", "dp", None),
        ),
        check_vma=False,
    )
```

profile of v0, /device:TPU:1, one launch (start us, length us, event | category | flops | bytes accessed | tf_op | source)
XLA Modules:
  0.0 228.2 jit_solution(13900909011576928776)
XLA Ops:
  7.2 0.0 copy-start
  7.2 0.9 copy.48
  8.1 0.1 reshape.219
  8.3 0.1 eq.39
  8.4 0.6 reduce-window.6
  9.0 0.2 slice_reduce_fusion
  9.2 0.1 fusion.51
  9.4 0.2 select_reduce_fusion.1
  9.5 0.2 fusion.48
  9.7 6.3 %gather_fusion = bf16[512,2048]{1,0:T(8,128)(2,1)} fusion(bf16[128,2048]{1,0:T(8,128)(2,1)} %param.11, s32[1024]{0:T(1024)S(1)} %pad_clamp_fusion.1), kind=kCustom, calls=%fused_computation.clone | custom fusion | bytes 4196352 | tf_op jit(solution)/shard_map/jit(_take)/gather | solution.py:33
  16.1 3.2 %select_select_fusion.1 = bf16[512,2048]{1,0:T(8,128)(2,1)} fusion(bf16[512,2048]{1,0:T(8,128)(2,1)} %gather_fusion, pred[512]{0:T(512)(128)(4,1)S(1)} %get-tuple-element.29, pred[512]{0:T(512)(128)(4,1)S(1)} %fusion.48), kind=kLoop, calls=%fused_computation.35 | loop fusion | flops 2097152 | bytes 4195328 | tf_op jit(solution)/shard_map/jit(_where)/select_n | solution.py:32
  19.3 8.6 %all-to-all-start = ((bf16[32,1,16,2048]{3,2,1,0:T(8,128)(2,1)}), bf16[32,1,16,2048]{3,2,1,0:T(8,128)(2,1)}, u32[]{:S(2)}, u32[]{:S(2)}) async-start(bf16[32,1,16,2048]{3,2,1,0:T(8,128)(2,1)} %bitcast.191), calls=%async_computation | async-start | bytes 4194304 | tf_op jit(solution)/shard_map/all_to_all | solution.py:36
  27.9 6.4 %gather_fusion.2 = bf16[512,2048]{1,0:T(8,128)(2,1)} fusion(bf16[128,2048]{1,0:T(8,128)(2,1)} %param.17, s32[1024]{0:T(1024)S(1)} %pad_clamp_fusion.1), kind=kCustom, calls=%fused_computation.2.clone | custom fusion | bytes 4196352 | tf_op jit(solution)/shard_map/jit(_take)/gather | solution.py:57
  34.3 0.1 copy.53
  34.4 0.1 broadcast_in_dim.73
  34.6 0.2 select_reduce_fusion
  34.7 3.7 %multiply_convert_fusion = bf16[512,2048]{1,0:T(8,128)(2,1)} fusion(bf16[512,2048]{1,0:T(8,128)(2,1)} %gather_fusion.2, f32[512]{0:T(512)S(1)} %select_reduce_fusion, pred[512]{0:T(512)(128)(4,1)S(1)} %get-tuple-element.29, pred[512]{0:T(512)(128)(4,1)S(1)} %fusion.48), kind=kLoop, calls=%fused_computation.9 | loop fusion | flops 5242880 | bytes 4197376 | tf_op jit(solution)/shard_map/convert_element_type | solution.py:59
  38.4 17.8 %all-to-all-done = bf16[32,1,16,2048]{3,2,1,0:T(8,128)(2,1)} async-done(((bf16[32,1,16,2048]{3,2,1,0:T(8,128)(2,1)}), bf16[32,1,16,2048]{3,2,1,0:T(8,128)(2,1)}, u32[]{:S(2)}, u32[]{:S(2)}) %all-to-all-start) | async-done | bytes 2097184 | tf_op jit(solution)/shard_map/all_to_all | solution.py:36
  56.3 5.2 %all-to-all-start.2 = ((bf16[32,1,16,2048]{3,2,1,0:T(8,128)(2,1)}), bf16[32,1,16,2048]{3,2,1,0:T(8,128)(2,1)}, u32[]{:S(2)}, u32[]{:S(2)}) async-start(bf16[32,1,16,2048]{3,2,1,0:T(8,128)(2,1)} %bitcast.192), calls=%async_computation.2 | async-start | bytes 4194304 | tf_op jit(solution)/shard_map/all_to_all | solution.py:61
  61.5 0.2 reduce-scatter.2.cloned.1.call-start
  61.7 5.6 %fusion.6 = f32[32,16,768]{2,1,0:T(8,128)} fusion(bf16[1,2048,768]{2,1,0:T(8,128)(2,1)} %param.15, bf16[32,1,16,2048]{3,2,1,0:T(8,128)(2,1)} %all-to-all-done), kind=kOutput, calls=%fused_computation.16 | convolution fusion | flops 1610612736 | bytes 6815744 | tf_op jit(solution)/shard_map/secd,edh->sech/dot_general | solution.py:40
  67.3 4.6 %fusion.10 = f32[32,16,768]{2,1,0:T(8,128)} fusion(bf16[1,2048,768]{2,1,0:T(8,128)(2,1)S(1)} %copy-done.2, bf16[32,1,16,2048]{3,2,1,0:T(8,128)(2,1)} %all-to-all-done), kind=kOutput, calls=%fused_computation.20 | convolution fusion | flops 1610612736 | bytes 6815744 | tf_op jit(solution)/shard_map/secd,edh->sech/dot_general | solution.py:37
  72.0 17.9 %all-to-all-done.2 = bf16[32,1,16,2048]{3,2,1,0:T(8,128)(2,1)} async-done(((bf16[32,1,16,2048]{3,2,1,0:T(8,128)(2,1)}), bf16[32,1,16,2048]{3,2,1,0:T(8,128)(2,1)}, u32[]{:S(2)}, u32[]{:S(2)}) %all-to-all-start.2) | async-done | bytes 2097184 | tf_op jit(solution)/shard_map/all_to_all | solution.py:61
  89.9 4.8 %fusion.34 = (bf16[32,1,16,768]{3,2,0,1:T(8,128)(2,1)S(1)}, bf16[32,1,16,768]{3,2,0,1:T(8,128)(2,1)S(1)}, bf16[32,1,16,768]{3,2,0,1:T(8,128)(2,1)S(1)}) fusion(f32[32,16,768]{2,1,0:T(8,128)} %fusion.6, f32[32,16,768]{2,1,0:T(8,128)} %fusion.10, bf16[1,2048,768]{2,1,0:T(8,128)(2,1)S(1)} %copy-done, bf16[32,1,16,2048]{3,2,1,0:T(8,128)(2,1)} %all-to-all-done.2), kind=kOutput, calls=%fused_computation.41 | convolution fusion | flops 1616904192 | bytes 10747904 | tf_op jit(solution)/shard_map/secd,edh->sech/dot_general | solution.py:62
  94.7 4.3 %fusion.17 = bf16[2048,1,1,768]{0,3,2,1:T(8,128)(2,1)S(1)} fusion(bf16[32,1,16,2048]{3,2,1,0:T(8,128)(2,1)} %all-to-all-done.2, bf16[32,1,16,768]{3,2,0,1:T(8,128)(2,1)S(1)} %get-tuple-element.32), kind=kOutput, calls=%fused_computation.25 | convolution fusion | flops 1612185600 | bytes 6029312 | tf_op jit(solution)/shard_map/secd,sech->deh/dot_general | solution.py:84
  99.0 3.4 %fusion.16 = bf16[2048,1,1,768]{0,3,2,1:T(8,128)(2,1)S(1)} fusion(bf16[32,1,16,2048]{3,2,1,0:T(8,128)(2,1)} %all-to-all-done, bf16[32,1,16,768]{3,2,0,1:T(8,128)(2,1)S(1)} %get-tuple-element.33), kind=kOutput, calls=%fused_computation.24 | convolution fusion | flops 1612185600 | bytes 6029312 | tf_op jit(solution)/shard_map/secd,sech->deh/dot_general | solution.py:77
  102.4 3.4 %fusion.15 = bf16[2048,1,1,768]{0,3,2,1:T(8,128)(2,1)S(1)} fusion(bf16[32,1,16,2048]{3,2,1,0:T(8,128)(2,1)} %all-to-all-done, bf16[32,1,16,768]{3,2,0,1:T(8,128)(2,1)S(1)} %get-tuple-element.31), kind=kOutput, calls=%fused_computation.23 | convolution fusion | flops 1612185600 | bytes 6029312 | tf_op jit(solution)/shard_map/secd,sech->deh/dot_general | solution.py:76
  105.9 4.5 %pad_maximum_fusion = bf16[2048,3,1,768]{0,3,2,1:T(8,128)(2,1)} fusion(bf16[2048,1,1,768]{0,3,2,1:T(8,128)(2,1)S(1)} %fusion.17, bf16[2048,1,1,768]{0,3,2,1:T(8,128)(2,1)S(1)} %fusion.16, bf16[2048,1,1,768]{0,3,2,1:T(8,128)(2,1)S(1)} %fusion.15), kind=kLoop, calls=%fused_computation.4 | loop fusion | flops 9437184 | bytes 18874368 | tf_op jit(solution)/shard_map/concatenate | solution.py:81
  110.3 0.0 reduce-scatter.2.cloned.1.call-update
  110.4 4.1 %fusion.4 = f32[32,16,2048]{2,1,0:T(8,128)S(1)} fusion(bf16[1,2048,768]{2,1,0:T(8,128)(2,1)} %param.15, bf16[32,1,16,768]{3,2,0,1:T(8,128)(2,1)} %copy-done.6), kind=kOutput, calls=%fused_computation.14 | convolution fusion | flops 1610612736 | bytes 8126464 | tf_op jit(solution)/shard_map/sech,edh->secd/dot_general | solution.py:68
  114.5 3.1 %fusion.23 = bf16[32,1,16,2048]{3,2,1,0:T(8,128)(2,1)} fusion(f32[32,16,2048]{2,1,0:T(8,128)S(1)} %fusion.4, bf16[1,2048,768]{2,1,0:T(8,128)(2,1)S(1)} %copy-done.3, bf16[32,1,16,768]{3,2,0,1:T(8,128)(2,1)S(1)} %copy-done.5), kind=kOutput, calls=%fused_computation.27 | convolution fusion | flops 1612709888 | bytes 10223616 | tf_op jit(solution)/shard_map/sech,edh->secd/dot_general | solution.py:66
  117.6 5.2 %all-to-all-start.3 = ((bf16[32,1,16,2048]{3,2,1,0:T(8,128)(2,1)}), bf16[32,1,16,2048]{3,2,1,0:T(8,128)(2,1)}, u32[]{:S(2)}, u32[]{:S(2)}) async-start(bf16[32,1,16,2048]{3,2,1,0:T(8,128)(2,1)} %fusion.23), calls=%async_computation.3 | async-start | bytes 4194304 | tf_op jit(solution)/shard_map/all_to_all | solution.py:70
  122.9 4.4 %fusion.20 = bf16[32,1,16,2048]{3,2,1,0:T(8,128)(2,1)} fusion(bf16[1,2048,768]{2,1,0:T(8,128)(2,1)S(1)} %copy-done, bf16[32,1,16,768]{3,2,0,1:T(8,128)(2,1)} %copy-done.7), kind=kOutput, calls=%fused_computation.26 | convolution fusion | flops 1611661312 | bytes 6029312 | tf_op jit(solution)/shard_map/sech,edh->secd/dot_general | solution.py:42
  127.2 24.0 %all-to-all-done.3 = bf16[32,1,16,2048]{3,2,1,0:T(8,128)(2,1)} async-done(((bf16[32,1,16,2048]{3,2,1,0:T(8,128)(2,1)}), bf16[32,1,16,2048]{3,2,1,0:T(8,128)(2,1)}, u32[]{:S(2)}, u32[]{:S(2)}) %all-to-all-start.3) | async-done | bytes 2097184 | tf_op jit(solution)/shard_map/all_to_all | solution.py:70
  151.3 5.2 %all-to-all-start.1 = ((bf16[32,1,16,2048]{3,2,1,0:T(8,128)(2,1)}), bf16[32,1,16,2048]{3,2,1,0:T(8,128)(2,1)}, u32[]{:S(2)}, u32[]{:S(2)}) async-start(bf16[32,1,16,2048]{3,2,1,0:T(8,128)(2,1)} %fusion.20), calls=%async_computation.1 | async-start | bytes 4194304 | tf_op jit(solution)/shard_map/all_to_all | solution.py:45
  156.5 5.3 %gather_fusion.3 = bf16[256,2048]{1,0:T(8,128)(2,1)} fusion(bf16[512,2048]{1,0:T(8,128)(2,1)} %bitcast.40, s32[1024]{0:T(1024)S(1)} %pad_clamp_fusion), kind=kCustom, calls=%fused_computation.3.clone | custom fusion | bytes 2098176 | tf_op jit(solution)/shard_map/jit(_take)/gather | solution.py:71
  161.8 23.1 %all-to-all-done.1 = bf16[32,1,16,2048]{3,2,1,0:T(8,128)(2,1)} async-done(((bf16[32,1,16,2048]{3,2,1,0:T(8,128)(2,1)}), bf16[32,1,16,2048]{3,2,1,0:T(8,128)(2,1)}, u32[]{:S(2)}, u32[]{:S(2)}) %all-to-all-start.1) | async-done | bytes 2097184 | tf_op jit(solution)/shard_map/all_to_all | solution.py:45
  184.9 5.3 %gather_fusion.1 = bf16[256,2048]{1,0:T(8,128)(2,1)} fusion(bf16[512,2048]{1,0:T(8,128)(2,1)} %bitcast.23, s32[1024]{0:T(1024)S(1)} %pad_clamp_fusion), kind=kCustom, calls=%fused_computation.1.clone | custom fusion | bytes 2098176 | tf_op jit(solution)/shard_map/jit(_take)/gather | solution.py:53
  190.2 3.5 %broadcast_select_fusion = (bf16[256,2048]{1,0:T(8,128)(2,1)}, f32[256,2048]{1,0:T(8,128)}) fusion(bf16[256,2048]{1,0:T(8,128)(2,1)} %gather_fusion.3, pred[256]{0:T(512)(128)(4,1)S(1)} %get-tuple-element.27, bf16[256,2048]{1,0:T(8,128)(2,1)} %gather_fusion.1), kind=kLoop, calls=%fused_computation.54 | loop fusion | flops 1572864 | bytes 5243136 | tf_op jit(solution)/shard_map/jit(_take)/select_n | solution.py:71
  193.7 3.5 %reshape.238 = f32[128,2,2048]{2,1,0:T(2,128)} reshape(f32[256,2048]{1,0:T(8,128)} %get-tuple-element.38) | data formatting | bytes 4194304 | tf_op jit(solution)/shard_map/reshape | solution.py:54
  197.2 2.5 %reshape.235 = bf16[128,2,2048]{2,1,0:T(2,128)(2,1)} reshape(bf16[256,2048]{1,0:T(8,128)(2,1)} %get-tuple-element.37) | data formatting | bytes 2097152 | tf_op jit(solution)/shard_map/reshape | solution.py:72
  199.7 4.6 %reduce = bf16[128,2048]{1,0:T(8,128)(2,1)} reduce(bf16[128,2,2048]{2,1,0:T(2,128)(2,1)} %reshape.235, bf16[]{:T(256)} %constant.48.clone.1), dimensions={1}, to_apply=%region_7.10.clone | reduce | flops 262144 | bytes 1572866 | tf_op jit(solution)/shard_map/reduce_sum | solution.py:72
  204.3 5.6 %multiply_reduce_fusion = bf16[128,2048]{1,0:T(8,128)(2,1)} fusion(f32[128,2,2048]{2,1,0:T(2,128)} %reshape.238, f32[128,2]{1,0:T(8,128)S(1)} %copy.53), kind=kLoop, calls=%fused_computation.36 | loop fusion | flops 786432 | bytes 2622464 | tf_op jit(solution)/shard_map/reduce_sum | solution.py:55
  209.9 4.5 %reduce-scatter.2.cloned.1.call-done = bf16[256,3,1,768]{0,3,2,1:T(8,128)(2,1)} async-done(((bf16[2048,3,1,768]{0,3,2,1:T(8,128)(2,1)}), bf16[256,3,1,768]{0,3,2,1:T(8,128)(2,1)}) %reduce-scatter.2.cloned.1.call-update) | async-done | bytes 1179664 | tf_op jit(solution)/shard_map/reduce_scatter | solution.py:80
  214.4 2.2 slice_bitcast_fusion
  216.6 1.9 copy.57
  218.5 1.9 copy.58
  220.5 0.9 copy.59
  (23 shorter events, 0.1 us)
Async XLA Ops:
  7.2 82.7 %copy-start = (bf16[1,2048,768]{2,1,0:T(8,128)(2,1)S(1)}, bf16[1,2048,768]{2,1,0:T(8,128)(2,1)}, u32[]{:S(2)}) copy-start(bf16[1,2048,768]{2,1,0:T(8,128)(2,1)} %param.16) | copy-start | bytes 9437188
  19.3 37.0 %all-to-all-start = ((bf16[32,1,16,2048]{3,2,1,0:T(8,128)(2,1)}), bf16[32,1,16,2048]{3,2,1,0:T(8,128)(2,1)}, u32[]{:S(2)}, u32[]{:S(2)}) async-start(bf16[32,1,16,2048]{3,2,1,0:T(8,128)(2,1)} %bitcast.191), calls=%async_computation | async-start | bytes 4194304 | tf_op jit(solution)/shard_map/all_to_all | solution.py:36
  27.9 6.4 %copy-start.1 = (f32[128,2]{0,1:T(2,128)S(1)}, f32[128,2]{0,1:T(2,128)}, u32[]{:S(2)}) copy-start(f32[128,2]{0,1:T(2,128)} %param.13) | copy-start | bytes 3076
  56.3 33.6 %all-to-all-start.2 = ((bf16[32,1,16,2048]{3,2,1,0:T(8,128)(2,1)}), bf16[32,1,16,2048]{3,2,1,0:T(8,128)(2,1)}, u32[]{:S(2)}, u32[]{:S(2)}) async-start(bf16[32,1,16,2048]{3,2,1,0:T(8,128)(2,1)} %bitcast.192), calls=%async_computation.2 | async-start | bytes 4194304 | tf_op jit(solution)/shard_map/all_to_all | solution.py:61
  61.5 153.0 %reduce-scatter.2.cloned.1.call-start = ((), (), s32[]{:S(2)}) async-start(), calls=%async_computation.5 | async-start | bytes 10616832 | tf_op jit(solution)/shard_map/reduce_scatter | solution.py:80
  61.7 5.6 %copy-start.2 = (bf16[1,2048,768]{2,1,0:T(8,128)(2,1)S(1)}, bf16[1,2048,768]{2,1,0:T(8,128)(2,1)}, u32[]{:S(2)}) copy-start(bf16[1,2048,768]{2,1,0:T(8,128)(2,1)} %param.14) | copy-start | bytes 9437188
  94.7 4.3 %copy-start.7 = (bf16[32,1,16,768]{3,2,0,1:T(8,128)(2,1)}, bf16[32,1,16,768]{3,2,0,1:T(8,128)(2,1)S(1)}, u32[]{:S(2)}) copy-start(bf16[32,1,16,768]{3,2,0,1:T(8,128)(2,1)S(1)} %get-tuple-element.32) | copy-start | bytes 2359300
  94.7 4.3 %copy-start.6 = (bf16[32,1,16,768]{3,2,0,1:T(8,128)(2,1)}, bf16[32,1,16,768]{3,2,0,1:T(8,128)(2,1)S(1)}, u32[]{:S(2)}) copy-start(bf16[32,1,16,768]{3,2,0,1:T(8,128)(2,1)S(1)} %get-tuple-element.33) | copy-start | bytes 2359300
  94.7 7.7 %copy-start.4 = (bf16[32,1,16,768]{3,2,0,1:T(8,128)(2,1)}, bf16[32,1,16,768]{3,2,0,1:T(8,128)(2,1)S(1)}, u32[]{:S(2)}) copy-start(bf16[32,1,16,768]{3,2,0,1:T(8,128)(2,1)S(1)} %get-tuple-element.31) | copy-start | bytes 2359300
  110.4 4.1 %copy-start.3 = (bf16[1,2048,768]{2,1,0:T(8,128)(2,1)S(1)}, bf16[1,2048,768]{2,1,0:T(8,128)(2,1)}, u32[]{:S(2)}) copy-start(bf16[1,2048,768]{2,1,0:T(8,128)(2,1)} %param.14) | copy-start | bytes 9437188
  110.4 4.1 %copy-start.5 = (bf16[32,1,16,768]{3,2,0,1:T(8,128)(2,1)S(1)}, bf16[32,1,16,768]{3,2,0,1:T(8,128)(2,1)}, u32[]{:S(2)}) copy-start(bf16[32,1,16,768]{3,2,0,1:T(8,128)(2,1)} %copy-done.4) | copy-start | bytes 2359300
  117.6 33.6 %all-to-all-start.3 = ((bf16[32,1,16,2048]{3,2,1,0:T(8,128)(2,1)}), bf16[32,1,16,2048]{3,2,1,0:T(8,128)(2,1)}, u32[]{:S(2)}, u32[]{:S(2)}) async-start(bf16[32,1,16,2048]{3,2,1,0:T(8,128)(2,1)} %fusion.23), calls=%async_computation.3 | async-start | bytes 4194304 | tf_op jit(solution)/shard_map/all_to_all | solution.py:70
  151.3 33.6 %all-to-all-start.1 = ((bf16[32,1,16,2048]{3,2,1,0:T(8,128)(2,1)}), bf16[32,1,16,2048]{3,2,1,0:T(8,128)(2,1)}, u32[]{:S(2)}, u32[]{:S(2)}) async-start(bf16[32,1,16,2048]{3,2,1,0:T(8,128)(2,1)} %fusion.20), calls=%async_computation.1 | async-start | bytes 4194304 | tf_op jit(solution)/shard_map/all_to_all | solution.py:45
Sparse Core Ops, SparseCore 0:
  110.5 103.9 reduce-scatter.1
where the time goes:
time: 229 us; the launch traced here: 228 us
  waiting for transfers between devices  87.5 us (38%)
  local copies, waits for them, and re-layouts  37.9 us (17%)
  matrix products  37.7 us (16%)
  other arithmetic  26.3 us (11%)
  starting transfers between devices  24.5 us (11%)
  between operations  14.3 us (6%)
    all_to_all x1, waiting for transfers between devices, local(): lax.all_to_all(dx_slot, 'expert', split_axis=0, concat_axis=0, tiled=True)  24 us
    all_to_all x1, waiting for transfers between devices, local(): lax.all_to_all(result, 'expert', split_axis=0, concat_axis=0, tiled=True)  23.1 us
    all_to_all x1, waiting for transfers between devices, local(): lax.all_to_all(dy_slot, 'expert', split_axis=0, concat_axis=0, tiled=True)  17.9 us
    all_to_all x1, waiting for transfers between devices, local(): lax.all_to_all(dispatched, 'expert', split_axis=0, concat_axis=0, tiled=T...  17.8 us
    all_to_all x1, starting transfers between devices, local(): lax.all_to_all(dispatched, 'expert', split_axis=0, concat_axis=0, tiled=T...  8.64 us
    gather x1, local copies, waits for them, and re-layouts, local(): jnp.take(out_grad, token_of_slot, axis=0)  6.39 us
    gather x1, local copies, waits for them, and re-layouts, local(): jnp.take(tokens, token_of_slot, axis=0)  6.35 us
    unnamed x21, local copies, waits for them, and re-layouts  5.84 us
  transfers between devices with their start and end apart: 5, of which 5 were waited for; matrix products, arithmetic and copies ran while one was open for 27% of the time, Pallas kernels for 0%

commit v1 on v0

v1 whole, which is shorter than its diff:
```python
import functools

import jax
import jax.numpy as jnp
from jax import lax
from jax.experimental import pallas as pl
from jax.experimental.pallas import tpu as pltpu
from jax.sharding import PartitionSpec as P

MESH = pl.DeviceIdType.MESH
F32 = jnp.float32
BF16 = jnp.bfloat16

NX, NY, NC = 4, 4, 2
CHIPS = NX * NY
PEERS = CHIPS * NC
NZ = 8
TOK = 128
TOP = 2
CAP = 16
SLOTS = PEERS * CAP
D = 2048
H = 768
SHARD = D // NZ
HALF = SHARD // 2
PIECES = 7


def dot(a, b):
    return jnp.dot(a, b, preferred_element_type=F32)


def dot_rhs_t(a, b):
    return lax.dot_general(a, b, (((1,), (1,)), ((), ())), preferred_element_type=F32)


def place(index):
    return index // (NY * NC), lax.rem(index // NC, NY), lax.rem(index, NC)


def offset(j):
    p = lax.rem(j * 7, CHIPS)
    return p // NY, lax.rem(p, NY)


def ahead(x, y, core, j):
    dx, dy = offset(j)
    return (lax.rem(x + dx, NX) * NY + lax.rem(y + dy, NY)) * NC + core


def behind(x, y, core, j):
    dx, dy = offset(j)
    return (lax.rem(x + NX - dx, NX) * NY + lax.rem(y + NY - dy, NY)) * NC + core


def rows_of(block):
    return pl.ds(pl.multiple_of(block * CAP, CAP), CAP)


def loop(low, high, body):
    def step(i, carry):
        body(i)
        return carry

    lax.fori_loop(low, high, step, 0)


def kernel(
    ids_ref, prob_ref, tok_hbm, og_hbm, wg_hbm, wu_hbm, wd_hbm,
    mixed_ref, tgrad_ref, gg_ref, gu_ref, gd_ref,
    tok, og, wg, wu, wd,
    xs, ds, xr, dr, hid, dg, du, ca, cb,
    ov, dxv, orv, dxr,
    sp, sq, rp, rq, acc,
    load_sem, xss, dss, oss, dxss, xrs, drs, ors, dxrs, pss, qss, prs, qrs,
):
    me = lax.axis_index("expert")
    z = lax.axis_index("dp")
    x, y, core = place(me)
    up = lax.rem(z + 1, NZ)
    down = lax.rem(z + NZ - 1, NZ)

    loads = [
        pltpu.make_async_copy(src, dst, load_sem.at[i])
        for i, (src, dst) in enumerate(
            [(tok_hbm, tok), (og_hbm, og), (wg_hbm.at[0], wg), (wu_hbm.at[0], wu), (wd_hbm.at[0], wd)]
        )
    ]
    for load in loads:
        load.start()

    barrier = pltpu.get_barrier_semaphore()

    def greet(i):
        pl.semaphore_signal(
            barrier, inc=1, device_id={"expert": lax.rem(me + i, PEERS)}, device_id_type=MESH
        )

    loop(1, PEERS, greet)
    for other in (up, down):
        pl.semaphore_signal(barrier, inc=1, device_id={"dp": other}, device_id_type=MESH)

    sub = lax.broadcasted_iota(jnp.int32, (TOK, TOK), 0)
    lane = lax.broadcasted_iota(jnp.int32, (TOK, TOK), 1)
    eye = sub == lane
    lane_f = lane.astype(F32)

    def to_col(row):
        return jnp.sum(jnp.where(eye, row, 0.0), axis=1, keepdims=True)

    def to_row(col):
        return jnp.sum(jnp.where(eye, col, 0.0), axis=0, keepdims=True)

    ids_f = ids_ref[...].astype(F32)
    probs = prob_ref[...]
    id_col = [to_col(ids_f[k : k + 1]) for k in range(TOP)]
    hot = [lane_f == id_col[k] for k in range(TOP)]
    chosen = jnp.where(hot[0] | hot[1], 1.0, 0.0).astype(BF16)
    earlier = jnp.where(lane < sub, 1.0, 0.0).astype(BF16)
    before = dot(earlier, chosen)
    slot_col = [
        id_col[k] * CAP + jnp.sum(jnp.where(hot[k], before, 0.0), axis=1, keepdims=True)
        for k in range(TOP)
    ]
    slot_row = [to_row(slot_col[k]) for k in range(TOP)]
    prob_row = [probs[k : k + 1] for k in range(TOP)]
    prob_col = [to_col(prob_row[k]) for k in range(TOP)]
    slot_of = lax.broadcasted_iota(jnp.int32, (SLOTS, TOK), 0).astype(F32)
    owner = [slot_of == slot_row[k] for k in range(TOP)]
    pick = jnp.where(owner[0] | owner[1], 1.0, 0.0).astype(BF16)
    slot_prob = jnp.sum(
        jnp.where(owner[0], prob_row[0], 0.0) + jnp.where(owner[1], prob_row[1], 0.0),
        axis=1,
        keepdims=True,
    )

    WIDE = 512

    def wide(n):
        return pl.ds(pl.multiple_of(n * WIDE, WIDE), WIDE)

    loads[0].wait()

    def build_x(n):
        xs[:, wide(n)] = dot(pick, tok[:, wide(n)]).astype(BF16)

    loop(0, D // WIDE, build_x)
    pl.semaphore_wait(barrier, PEERS - 1 + 2)

    def to_expert(src, dst, send_sem, recv_sem, j, t):
        peer = ahead(x, y, t, j)
        return pltpu.make_async_remote_copy(
            src.at[rows_of(peer)],
            dst.at[rows_of(j * NC + core)],
            send_sem.at[t * CHIPS + j],
            recv_sem.at[j * NC + core],
            device_id={"expert": peer},
            device_id_type=MESH,
        )

    def own_block(src, dst, recv_sem):
        return pltpu.make_async_copy(src.at[rows_of(me)], dst.at[rows_of(core)], recv_sem.at[core])

    def dispatch(src, dst, send_sem, recv_sem, t):
        @pl.when(core == t)
        def _():
            own_block(src, dst, recv_sem).start()

        @pl.when(core != t)
        def _():
            to_expert(src, dst, send_sem, recv_sem, 0, t).start()

        loop(1, CHIPS, lambda j: to_expert(src, dst, send_sem, recv_sem, j, t).start())

    dispatch(xs, xr, xss, xrs, 0)
    loads[1].wait()

    def build_dy(n):
        ds[:, wide(n)] = (dot(pick, og[:, wide(n)]) * slot_prob).astype(BF16)

    loop(0, D // WIDE, build_dy)
    dispatch(ds, dr, dss, drs, 0)
    dispatch(xs, xr, xss, xrs, 1)
    dispatch(ds, dr, dss, drs, 1)

    def arrived(dst, recv_sem, i):
        pltpu.make_async_copy(dst.at[rows_of(i)], dst.at[rows_of(i)], recv_sem.at[i]).wait()

    TILE = 256
    MX = 256

    def tile(n):
        return pl.ds(pl.multiple_of(n * TILE, TILE), TILE)

    loads[2].wait()
    loads[3].wait()

    def forward(m):
        loop(0, MX // CAP, lambda i: arrived(xr, xrs, m * (MX // CAP) + i))
        rows = pl.ds(pl.multiple_of(m * MX, MX), MX)

        def columns(n):
            g = dot(xr[rows, :], wg[:, tile(n)])
            u = dot(xr[rows, :], wu[:, tile(n)])
            s = 1.0 / (1.0 + jnp.exp(-g))
            gs = g * s
            hid[rows, tile(n)] = (gs * u).astype(BF16)
            cb[rows, tile(n)] = gs
            ca[rows, tile(n)] = u * s * (1.0 + g * (1.0 - s))

        loop(0, H // TILE, columns)

    loop(0, SLOTS // MX, forward)

    loads[4].wait()
    MD = 128

    def backward(m):
        loop(0, MD // CAP, lambda i: arrived(dr, drs, m * (MD // CAP) + i))
        rows = pl.ds(pl.multiple_of(m * MD, MD), MD)

        def columns(n):
            dh = dot(dr[rows, :], wd[:, tile(n)])
            dg[rows, tile(n)] = (dh * ca[rows, tile(n)]).astype(BF16)
            du[rows, tile(n)] = (dh * cb[rows, tile(n)]).astype(BF16)

        loop(0, H // TILE, columns)

    loop(0, SLOTS // MD, backward)

    def own_part(shard, half, out):
        cols = pl.ds(pl.multiple_of(shard * SHARD + half * HALF, HALF), HALF)
        xt = jnp.transpose(xr[:, cols])
        out[0:HALF] = dot(xt, dg[...])
        out[HALF : 2 * HALF] = dot(xt, du[...])
        dt = jnp.transpose(dr[:, cols])
        out[2 * HALF : 3 * HALF] = dot(dt, hid[...])

    def shard_up(k):
        return lax.rem(z + 4 - (k + 1) // 2 + NZ, NZ), lax.rem(k + 1, 2)

    def shard_down(k):
        return lax.rem(z - 4 + (k + 1) // 2 + NZ, NZ), lax.rem(k, 2)

    def pass_on(src, dst, send_sem, recv_sem, k, to):
        return pltpu.make_async_remote_copy(
            src, dst.at[k], send_sem.at[k], recv_sem.at[k], device_id={"dp": to}, device_id_type=MESH
        )

    ways = (
        (shard_up, sp, rp, pss, prs, up),
        (shard_down, sq, rq, qss, qrs, down),
    )

    def first(k):
        for which, staged, got, send_sem, recv_sem, to in ways:
            shard, half = which(k)
            own_part(shard, half, acc)
            staged[k] = acc[...].astype(BF16)
            pass_on(staged.at[k], got, send_sem, recv_sem, k, to).start()

    loop(0, 2, first)

    def to_token(src, dst, send_sem, recv_sem, i):
        j, c = i // NC, lax.rem(i, NC)
        peer = behind(x, y, c, j)
        return pltpu.make_async_remote_copy(
            src.at[rows_of(i)],
            dst.at[rows_of(me)],
            send_sem.at[i],
            recv_sem.at[me],
            device_id={"expert": peer},
            device_id_type=MESH,
        )

    def give_back(src, dst, send_sem, recv_sem, i):
        @pl.when(i == core)
        def _():
            pltpu.make_async_copy(src.at[rows_of(i)], dst.at[rows_of(me)], recv_sem.at[me]).start()

        @pl.when(i != core)
        def _():
            to_token(src, dst, send_sem, recv_sem, i).start()

    def outputs(m):
        rows = pl.ds(pl.multiple_of(m * MD, MD), MD)

        def columns(n):
            ov[rows, tile(n)] = dot_rhs_t(hid[rows, :], wd[tile(n), :]).astype(BF16)
            dxv[rows, tile(n)] = (
                dot_rhs_t(dg[rows, :], wg[tile(n), :]) + dot_rhs_t(du[rows, :], wu[tile(n), :])
            ).astype(BF16)

        loop(0, D // TILE, columns)

        def send(i):
            give_back(ov, orv, oss, ors, m * (MD // CAP) + i)
            give_back(dxv, dxr, dxss, dxrs, m * (MD // CAP) + i)

        loop(0, MD // CAP, send)

    def later(k):
        for which, staged, got, send_sem, recv_sem, to in ways:
            shard, half = which(k)
            own_part(shard, half, acc)
            pass_on(got.at[k - 2], got, send_sem, recv_sem, k - 2, to).wait_recv()
            got[k - 2] = (acc[...] + got[k - 2].astype(F32)).astype(BF16)
            pass_on(got.at[k - 2], got, send_sem, recv_sem, k, to).start()

    def outputs_and_later(k):
        outputs(k - 2)
        later(k)

    loop(2, 2 + SLOTS // MD, outputs_and_later)
    loop(2 + SLOTS // MD, PIECES, later)

    loop(0, PEERS, lambda i: arrived(orv, ors, i))
    loop(0, PEERS, lambda i: arrived(dxr, dxrs, i))
    slot_lane = lax.broadcasted_iota(jnp.int32, (TOK, SLOTS), 1).astype(F32)
    route = [slot_lane == slot_col[k] for k in range(TOP)]
    one = [jnp.where(route[k], 1.0, 0.0).astype(BF16) for k in range(TOP)]
    either = jnp.where(route[0] | route[1], 1.0, 0.0).astype(BF16)

    def combine(n):
        mixed_ref[:, wide(n)] = (
            dot(one[0], orv[:, wide(n)]) * prob_col[0] + dot(one[1], orv[:, wide(n)]) * prob_col[1]
        ).astype(BF16)
        tgrad_ref[:, wide(n)] = dot(either, dxr[:, wide(n)]).astype(BF16)

    loop(0, D // WIDE, combine)

    for half, (k_up, k_down) in enumerate(((5, 6), (6, 5))):
        own_part(z, half, acc)
        pass_on(rp.at[k_up], rp, pss, prs, k_up, up).wait_recv()
        pass_on(rq.at[k_down], rq, qss, qrs, k_down, down).wait_recv()
        for w, out in enumerate((gg_ref, gu_ref, gd_ref)):
            rows = pl.ds(w * HALF, HALF)
            out[0, half * HALF : (half + 1) * HALF] = (
                acc[rows] + rp[k_up, rows].astype(F32) + rq[k_down, rows].astype(F32)
            ).astype(BF16)

    def sent(src, dst, send_sem, recv_sem, i):
        to_expert(src, dst, send_sem, recv_sem, lax.rem(i, CHIPS), i // CHIPS).wait_send()

    def all_sent(i):
        @pl.when(i != core * CHIPS)
        def _():
            sent(xs, xr, xss, xrs, i)
            sent(ds, dr, dss, drs, i)

        @pl.when(i != core)
        def _():
            to_token(ov, orv, oss, ors, i).wait_send()
            to_token(dxv, dxr, dxss, dxrs, i).wait_send()

    loop(0, PEERS, all_sent)

    def passed(k):
        pass_on(rp.at[k], rp, pss, prs, k, up).wait_send()
        pass_on(rq.at[k], rq, qss, qrs, k, down).wait_send()

    loop(0, PIECES, passed)


def local(tokens, expert_ids, gate_probs, w_gate, w_up, w_down, out_grad):
    vmem = pl.BlockSpec(memory_space=pltpu.VMEM)
    hbm = pl.BlockSpec(memory_space=pl.ANY)
    dma = pltpu.SemaphoreType.DMA
    slots = lambda: pltpu.VMEM((SLOTS, D), BF16)
    acts = lambda dtype: pltpu.VMEM((SLOTS, H), dtype)
    return pl.pallas_call(
        kernel,
        out_shape=(
            jax.ShapeDtypeStruct((TOK, D), BF16),
            jax.ShapeDtypeStruct((TOK, D), BF16),
            jax.ShapeDtypeStruct((1, SHARD, H), BF16),
            jax.ShapeDtypeStruct((1, SHARD, H), BF16),
            jax.ShapeDtypeStruct((1, SHARD, H), BF16),
        ),
        in_specs=[vmem, vmem] + [hbm] * 5,
        out_specs=(vmem,) * 5,
        scratch_shapes=[
            pltpu.VMEM((TOK, D), BF16),
            pltpu.VMEM((TOK, D), BF16),
            pltpu.VMEM((D, H), BF16),
            pltpu.VMEM((D, H), BF16),
            pltpu.VMEM((D, H), BF16),
            slots(), slots(), slots(), slots(),
            acts(BF16), acts(BF16), acts(BF16), acts(F32), acts(F32),
            slots(), slots(), slots(), slots(),
            pltpu.VMEM((2, 3 * HALF, H), BF16),
            pltpu.VMEM((2, 3 * HALF, H), BF16),
            pltpu.VMEM((PIECES, 3 * HALF, H), BF16),
            pltpu.VMEM((PIECES, 3 * HALF, H), BF16),
            pltpu.VMEM((3 * HALF, H), F32),
            dma((5,)),
            dma((PEERS,)), dma((PEERS,)), dma((PEERS,)), dma((PEERS,)),
            dma((PEERS,)), dma((PEERS,)), dma((PEERS,)), dma((PEERS,)),
            dma((PIECES,)), dma((PIECES,)), dma((PIECES,)), dma((PIECES,)),
        ],
        compiler_params=pltpu.CompilerParams(
            collective_id=0, has_side_effects=True, vmem_limit_bytes=62 * 2**20
        ),
        name="expert_layer",
    )(expert_ids.T, gate_probs.T, tokens, out_grad, w_gate, w_up, w_down)


def solution(mesh):
    placed = (
        P(("dp", "expert"), None),
        P(("dp", "expert"), None),
        P(("dp", "expert"), None),
        P("expert", None, None),
        P("expert", None, None),
        P("expert", None, None),
        P(("dp", "expert"), None),
    )
    return jax.shard_map(
        local,
        mesh=mesh,
        in_specs=placed,
        out_specs=(
            P(("dp", "expert"), None),
            P(("dp", "expert"), None),
            P("expert", "dp", None),
            P("expert", "dp", None),
            P("expert", "dp", None),
        ),
        check_vma=False,
    )
```

time: 229 us -> 146 us (0.64)
  Pallas kernels: 0 us -> 136 us
  waiting for transfers between devices: 87.5 us -> 0 us
  matrix products: 37.7 us -> 0 us
  local copies, waits for them, and re-layouts: 37.9 us -> 7.1 us
  other arithmetic: 26.3 us -> 0 us
  starting transfers between devices: 24.5 us -> 0 us
  between operations: 14.3 us -> 0.66 us
    pallas_call x0 -> x1, Pallas kernels: none -> 136 us  [local(): pl.pallas_call(kernel, out_shape=(jax.ShapeDtypeStruct((TOK, D), BF16), j...]
    all_to_all x4 -> x0, waiting for transfers between devices: 82.9 us -> none  [the longest x1 24 us: local(): lax.all_to_all(dx_slot, 'expert', split_axis=0, concat_axis=0, tiled=True)]
    dot_general x9 -> x0, matrix products: 37.7 us -> none  [the longest x1 5.6 us: local(): jnp.einsum('secd,edh->sech', expert_received, w_up, preferred_element_typ...]
    all_to_all x4 -> x0, starting transfers between devices: 24.3 us -> none  [the longest x1 8.64 us: local(): lax.all_to_all(dispatched, 'expert', split_axis=0, concat_axis=0, tiled=T...]
    gather x4 -> x0, local copies, waits for them, and re-layouts: 23.2 us -> none  [the longest x1 6.39 us: local(): jnp.take(out_grad, token_of_slot, axis=0)]
    reduce_sum x5 -> x0, other arithmetic: 10.6 us -> none  [the longest x1 5.64 us: local(): jnp.sum(picked * gate_probs[:, :, None], axis=1).astype(jnp.bfloat16)]
    select_n x3 -> x0, other arithmetic: 6.69 us -> none  [the longest x1 3.48 us: local(): jnp.take(dx_back.reshape(slot_total, width), slot, axis=0)]
    reshape x3 -> x0, local copies, waits for them, and re-layouts: 6.19 us -> none  [the longest x1 3.53 us: local(): picked = picked.reshape(token_count, top_count, width)]
  transfers between devices with their start and end apart: 5 -> 0, of which waited for: 5 -> 0; matrix products, arithmetic and copies ran while one was open for 27% -> 0% of each run, Pallas kernels for 0% -> 0%
where the time goes in v1:
time: 146 us; the launch traced here: 144 us
  Pallas kernels  136 us (93%)
  local copies, waits for them, and re-layouts  7.1 us (5%)
    pallas_call x1, Pallas kernels, local(): pl.pallas_call(kernel, out_shape=(jax.ShapeDtypeStruct((TOK, D), BF16), j...  136 us
    unnamed x9, local copies, waits for them, and re-layouts  7.1 us

profile of v1, /device:TPU:1, one launch (start us, length us, event | category | flops | bytes accessed | tf_op | source)
XLA Modules:
  0.0 143.7 jit_solution(1466269559917567591)
XLA Ops:
  0.6 136.0 %expert_layer.1 = (bf16[128,2048]{1,0:T(8,128)(2,1)}, bf16[128,2048]{1,0:T(8,128)(2,1)}, bf16[1,256,768]{2,1,0:T(8,128)(2,1)}, bf16[1,256,768]{2,1,0:T(8,128)(2,1)}, bf16[1,256,768]{2,1,0:T(8,128)(2,1)}) custom-call(s32[2,128]{1,0:T(2,128)} %bitcast.2, f32[2,128]{1,0:T(2,128)} %bitcast.3, bf16[128,2048]{1,0:T(8,128)(2,1)} %tok_hbm.1, ...), custom_call_target="tpu_custom_call" | custom-call | tf_op jit(solution)/shard_map/expert_layer/pallas_call | solution.py:371
  136.6 0.0 copy-start.1
  136.6 0.0 copy-start
  136.6 2.0 %copy.17 = bf16[128,2048]{1,0:T(8,128)(2,1)} copy(bf16[128,2048]{1,0:T(8,128)(2,1)} %get-tuple-element.10) | data formatting | bytes 1048576
  138.6 1.9 %copy.18 = bf16[128,2048]{1,0:T(8,128)(2,1)} copy(bf16[128,2048]{1,0:T(8,128)(2,1)} %get-tuple-element.11) | data formatting | bytes 1048576
  140.5 1.8 %copy.19 = bf16[1,256,768]{2,1,0:T(8,128)(2,1)} copy(bf16[1,256,768]{2,1,0:T(8,128)(2,1)} %get-tuple-element.12) | data formatting | bytes 786432
  142.2 0.0 copy-done.1
  142.2 0.7 copy.20
  143.0 0.0 copy-done
  143.0 0.7 copy.21
Async XLA Ops:
  136.6 5.6 %copy-start.1 = (bf16[1,256,768]{2,1,0:T(8,128)(2,1)S(1)}, bf16[1,256,768]{2,1,0:T(8,128)(2,1)}, u32[]{:S(2)}) copy-start(bf16[1,256,768]{2,1,0:T(8,128)(2,1)} %get-tuple-element.13) | copy-start | bytes 1179652
  136.6 6.4 %copy-start = (bf16[1,256,768]{2,1,0:T(8,128)(2,1)S(1)}, bf16[1,256,768]{2,1,0:T(8,128)(2,1)}, u32[]{:S(2)}) copy-start(bf16[1,256,768]{2,1,0:T(8,128)(2,1)} %get-tuple-element.14) | copy-start | bytes 1179652

commit v2 on v1

--- a/solution.py
+++ b/solution.py
@@ -38,18 +38,19 @@
     return index // (NY * NC), lax.rem(index // NC, NY), lax.rem(index, NC)
 
 
-def offset(j):
+def offset(j, core):
     p = lax.rem(j * 7, CHIPS)
-    return p // NY, lax.rem(p, NY)
-
-
-def ahead(x, y, core, j):
-    dx, dy = offset(j)
+    a, b = p // NY, lax.rem(p, NY)
+    return a + core * (b - a), b + core * (a - b)
+
+
+def ahead(x, y, own_core, core, j):
+    dx, dy = offset(j, own_core)
     return (lax.rem(x + dx, NX) * NY + lax.rem(y + dy, NY)) * NC + core
 
 
 def behind(x, y, core, j):
-    dx, dy = offset(j)
+    dx, dy = offset(j, core)
     return (lax.rem(x + NX - dx, NX) * NY + lax.rem(y + NY - dy, NY)) * NC + core
 
 
@@ -67,12 +68,12 @@
 
 def kernel(
     ids_ref, prob_ref, tok_hbm, og_hbm, wg_hbm, wu_hbm, wd_hbm,
-    mixed_ref, tgrad_ref, gg_ref, gu_ref, gd_ref,
+    mixed_hbm, tgrad_hbm, gg_hbm, gu_hbm, gd_hbm,
     tok, og, wg, wu, wd,
     xs, ds, xr, dr, hid, dg, du, ca, cb,
     ov, dxv, orv, dxr,
-    sp, sq, rp, rq, acc,
-    load_sem, xss, dss, oss, dxss, xrs, drs, ors, dxrs, pss, qss, prs, qrs,
+    sp, sq, rp, rq, acc, mixed, tgrad, grads,
+    load_sem, store_sem, xss, dss, oss, dxss, xrs, drs, ors, dxrs, pss, qss, prs, qrs,
 ):
     me = lax.axis_index("expert")
     z = lax.axis_index("dp")
@@ -148,7 +149,7 @@
     pl.semaphore_wait(barrier, PEERS - 1 + 2)
 
     def to_expert(src, dst, send_sem, recv_sem, j, t):
-        peer = ahead(x, y, t, j)
+        peer = ahead(x, y, core, t, j)
         return pltpu.make_async_remote_copy(
             src.at[rows_of(peer)],
             dst.at[rows_of(j * NC + core)],
@@ -228,13 +229,13 @@
 
     loop(0, SLOTS // MD, backward)
 
-    def own_part(shard, half, out):
+    right_sides = (dg, du, hid)
+
+    def left_sides(shard, half):
         cols = pl.ds(pl.multiple_of(shard * SHARD + half * HALF, HALF), HALF)
         xt = jnp.transpose(xr[:, cols])
-        out[0:HALF] = dot(xt, dg[...])
-        out[HALF : 2 * HALF] = dot(xt, du[...])
         dt = jnp.transpose(dr[:, cols])
-        out[2 * HALF : 3 * HALF] = dot(dt, hid[...])
+        return xt, xt, dt
 
     def shard_up(k):
         return lax.rem(z + 4 - (k + 1) // 2 + NZ, NZ), lax.rem(k + 1, 2)
@@ -242,9 +243,17 @@
     def shard_down(k):
         return lax.rem(z - 4 + (k + 1) // 2 + NZ, NZ), lax.rem(k, 2)
 
-    def pass_on(src, dst, send_sem, recv_sem, k, to):
+    def third(w):
+        return pl.ds(w * HALF, HALF)
+
+    def pass_on(src, slot, dst, send_sem, recv_sem, k, w, to):
         return pltpu.make_async_remote_copy(
-            src, dst.at[k], send_sem.at[k], recv_sem.at[k], device_id={"dp": to}, device_id_type=MESH
+            src.at[slot, third(w)],
+            dst.at[k, third(w)],
+            send_sem.at[k * 3 + w],
+            recv_sem.at[k * 3 + w],
+            device_id={"dp": to},
+            device_id_type=MESH,
         )
 
     ways = (
@@ -253,11 +262,11 @@
     )
 
     def first(k):
-        for which, staged, got, send_sem, recv_sem, to in ways:
-            shard, half = which(k)
-            own_part(shard, half, acc)
-            staged[k] = acc[...].astype(BF16)
-            pass_on(staged.at[k], got, send_sem, recv_sem, k, to).start()
+        lefts = [left_sides(*way[0](k)) for way in ways]
+        for w in range(3):
+            for left, (_, staged, got, send_sem, recv_sem, to) in zip(lefts, ways):
+                staged[k, third(w)] = dot(left[w], right_sides[w][...]).astype(BF16)
+                pass_on(staged, k, got, send_sem, recv_sem, k, w, to).start()
 
     loop(0, 2, first)
 
@@ -300,12 +309,13 @@
         loop(0, MD // CAP, send)
 
     def later(k):
-        for which, staged, got, send_sem, recv_sem, to in ways:
-            shard, half = which(k)
-            own_part(shard, half, acc)
-            pass_on(got.at[k - 2], got, send_sem, recv_sem, k - 2, to).wait_recv()
-            got[k - 2] = (acc[...] + got[k - 2].astype(F32)).astype(BF16)
-            pass_on(got.at[k - 2], got, send_sem, recv_sem, k, to).start()
+        lefts = [left_sides(*way[0](k)) for way in ways]
+        for w in range(3):
+            for left, (_, staged, got, send_sem, recv_sem, to) in zip(lefts, ways):
+                part = dot(left[w], right_sides[w][...])
+                pass_on(got, k - 2, got, send_sem, recv_sem, k - 2, w, to).wait_recv()
+                got[k - 2, third(w)] = (part + got[k - 2, third(w)].astype(F32)).astype(BF16)
+                pass_on(got, k - 2, got, send_sem, recv_sem, k, w, to).start()
 
     def outputs_and_later(k):
         outputs(k - 2)
@@ -322,22 +332,34 @@
     either = jnp.where(route[0] | route[1], 1.0, 0.0).astype(BF16)
 
     def combine(n):
-        mixed_ref[:, wide(n)] = (
+        mixed[:, wide(n)] = (
             dot(one[0], orv[:, wide(n)]) * prob_col[0] + dot(one[1], orv[:, wide(n)]) * prob_col[1]
         ).astype(BF16)
-        tgrad_ref[:, wide(n)] = dot(either, dxr[:, wide(n)]).astype(BF16)
+        tgrad[:, wide(n)] = dot(either, dxr[:, wide(n)]).astype(BF16)
 
     loop(0, D // WIDE, combine)
-
-    for half, (k_up, k_down) in enumerate(((5, 6), (6, 5))):
-        own_part(z, half, acc)
-        pass_on(rp.at[k_up], rp, pss, prs, k_up, up).wait_recv()
-        pass_on(rq.at[k_down], rq, qss, qrs, k_down, down).wait_recv()
-        for w, out in enumerate((gg_ref, gu_ref, gd_ref)):
-            rows = pl.ds(w * HALF, HALF)
-            out[0, half * HALF : (half + 1) * HALF] = (
-                acc[rows] + rp[k_up, rows].astype(F32) + rq[k_down, rows].astype(F32)
+    stores = [
+        pltpu.make_async_copy(mixed, mixed_hbm, store_sem.at[0]),
+        pltpu.make_async_copy(tgrad, tgrad_hbm, store_sem.at[1]),
+    ]
+    for store in stores:
+        store.start()
+
+    for half in range(2):
+        left = left_sides(z, half)
+        for w in range(3):
+            acc[half, third(w)] = dot(left[w], right_sides[w][...])
+    for w, out in enumerate((gg_hbm, gu_hbm, gd_hbm)):
+        for k in (PIECES - 2, PIECES - 1):
+            pass_on(rp, k, rp, pss, prs, k, w, up).wait_recv()
+            pass_on(rq, k, rq, qss, qrs, k, w, down).wait_recv()
+        for half, (k_up, k_down) in enumerate(((5, 6), (6, 5))):
+            grads[w, half * HALF : (half + 1) * HALF] = (
+                acc[half, third(w)] + rp[k_up, third(w)].astype(F32) + rq[k_down, third(w)].astype(F32)
             ).astype(BF16)
+        store = pltpu.make_async_copy(grads.at[w], out.at[0], store_sem.at[2 + w])
+        store.start()
+        stores.append(store)
 
     def sent(src, dst, send_sem, recv_sem, i):
         to_expert(src, dst, send_sem, recv_sem, lax.rem(i, CHIPS), i // CHIPS).wait_send()
@@ -356,10 +378,28 @@
     loop(0, PEERS, all_sent)
 
     def passed(k):
-        pass_on(rp.at[k], rp, pss, prs, k, up).wait_send()
-        pass_on(rq.at[k], rq, qss, qrs, k, down).wait_send()
+        for w in range(3):
+            pass_on(rp, k, rp, pss, prs, k, w, up).wait_send()
+            pass_on(rq, k, rq, qss, qrs, k, w, down).wait_send()
 
     loop(0, PIECES, passed)
+    for store in stores:
+        store.wait()
+
+
+def hand_on(*refs):
+    count = (len(refs) - 2) // 3
+    srcs, dsts, bufs = (refs[i * count : (i + 1) * count] for i in range(3))
+    in_sem, out_sem = refs[3 * count :]
+    ins = [pltpu.make_async_copy(s, b, in_sem.at[i]) for i, (s, b) in enumerate(zip(srcs, bufs))]
+    outs = [pltpu.make_async_copy(b, d, out_sem.at[i]) for i, (b, d) in enumerate(zip(bufs, dsts))]
+    for copy in ins:
+        copy.start()
+    for copy, then in zip(ins, outs):
+        copy.wait()
+        then.start()
+    for copy in outs:
+        copy.wait()
 
 
 def local(tokens, expert_ids, gate_probs, w_gate, w_up, w_down, out_grad):
@@ -368,17 +408,18 @@
     dma = pltpu.SemaphoreType.DMA
     slots = lambda: pltpu.VMEM((SLOTS, D), BF16)
     acts = lambda dtype: pltpu.VMEM((SLOTS, H), dtype)
-    return pl.pallas_call(
+    shapes = (
+        jax.ShapeDtypeStruct((TOK, D), BF16),
+        jax.ShapeDtypeStruct((TOK, D), BF16),
+        jax.ShapeDtypeStruct((1, SHARD, H), BF16),
+        jax.ShapeDtypeStruct((1, SHARD, H), BF16),
+        jax.ShapeDtypeStruct((1, SHARD, H), BF16),
+    )
+    results = pl.pallas_call(
         kernel,
-        out_shape=(
-            jax.ShapeDtypeStruct((TOK, D), BF16),
-            jax.ShapeDtypeStruct((TOK, D), BF16),
-            jax.ShapeDtypeStruct((1, SHARD, H), BF16),
-            jax.ShapeDtypeStruct((1, SHARD, H), BF16),
-            jax.ShapeDtypeStruct((1, SHARD, H), BF16),
-        ),
+        out_shape=shapes,
         in_specs=[vmem, vmem] + [hbm] * 5,
-        out_specs=(vmem,) * 5,
+        out_specs=(hbm,) * 5,
         scratch_shapes=[
             pltpu.VMEM((TOK, D), BF16),
             pltpu.VMEM((TOK, D), BF16),
@@ -392,17 +433,28 @@
             pltpu.VMEM((2, 3 * HALF, H), BF16),
             pltpu.VMEM((PIECES, 3 * HALF, H), BF16),
             pltpu.VMEM((PIECES, 3 * HALF, H), BF16),
-            pltpu.VMEM((3 * HALF, H), F32),
-            dma((5,)),
+            pltpu.VMEM((2, 3 * HALF, H), F32),
+            pltpu.VMEM((TOK, D), BF16),
+            pltpu.VMEM((TOK, D), BF16),
+            pltpu.VMEM((3, SHARD, H), BF16),
+            dma((5,)), dma((5,)),
             dma((PEERS,)), dma((PEERS,)), dma((PEERS,)), dma((PEERS,)),
             dma((PEERS,)), dma((PEERS,)), dma((PEERS,)), dma((PEERS,)),
-            dma((PIECES,)), dma((PIECES,)), dma((PIECES,)), dma((PIECES,)),
+            dma((PIECES * 3,)), dma((PIECES * 3,)), dma((PIECES * 3,)), dma((PIECES * 3,)),
         ],
         compiler_params=pltpu.CompilerParams(
             collective_id=0, has_side_effects=True, vmem_limit_bytes=62 * 2**20
         ),
         name="expert_layer",
     )(expert_ids.T, gate_probs.T, tokens, out_grad, w_gate, w_up, w_down)
+    return pl.pallas_call(
+        hand_on,
+        out_shape=shapes,
+        in_specs=[hbm] * 5,
+        out_specs=(hbm,) * 5,
+        scratch_shapes=[pltpu.VMEM(shape.shape, shape.dtype) for shape in shapes] + [dma((5,)), dma((5,))],
+        name="hand_on",
+    )(*results)
 
 
 def solution(mesh):

time: 146 us -> 138 us (0.945); the launches traced: 144 us -> 138 us
  local copies, waits for them, and re-layouts: 7.1 us -> 0 us
    unnamed x9 -> x0, local copies, waits for them, and re-layouts: 7.1 us -> none
    pallas_call x1 -> x2, Pallas kernels: 136 us -> 137 us  [the longest x1 135 us: local(): pl.pallas_call(kernel, out_shape=shapes, in_specs=[vmem, vmem] + [hbm] *...]
where the time goes in v2:
time: 138 us
  Pallas kernels  137 us (99%)
    pallas_call x1, Pallas kernels, local(): pl.pallas_call(kernel, out_shape=shapes, in_specs=[vmem, vmem] + [hbm] *...  135 us

profile of v2, /device:TPU:1, one launch (start us, length us, event | category | flops | bytes accessed | tf_op | source)
XLA Modules:
  0.0 137.9 jit_solution(14035162407306120642)
XLA Ops:
  0.6 134.8 %expert_layer.1 = (bf16[128,2048]{1,0:T(8,128)(2,1)}, bf16[128,2048]{1,0:T(8,128)(2,1)}, bf16[1,256,768]{2,1,0:T(8,128)(2,1)}, bf16[1,256,768]{2,1,0:T(8,128)(2,1)}, bf16[1,256,768]{2,1,0:T(8,128)(2,1)}) custom-call(s32[2,128]{1,0:T(2,128)} %bitcast.2, f32[2,128]{1,0:T(2,128)} %bitcast.3, bf16[128,2048]{1,0:T(8,128)(2,1)} %tok_hbm.1, ...), custom_call_target="tpu_custom_call" | custom-call | tf_op jit(solution)/shard_map/expert_layer/pallas_call | solution.py:418
  135.4 2.5 %hand_on.1 = (bf16[128,2048]{1,0:T(8,128)(2,1)}, bf16[128,2048]{1,0:T(8,128)(2,1)}, bf16[1,256,768]{2,1,0:T(8,128)(2,1)}, bf16[1,256,768]{2,1,0:T(8,128)(2,1)}, bf16[1,256,768]{2,1,0:T(8,128)(2,1)}) custom-call(bf16[128,2048]{1,0:T(8,128)(2,1)} %get-tuple-element.10.refs_0_, bf16[128,2048]{1,0:T(8,128)(2,1)} %get-tuple-element.11.refs_1_, ...), custom_call_target="tpu_custom_call" | custom-call | tf_op jit(solution)/shard_map/hand_on/pallas_call | solution.py:450

commit v3 on v2

--- a/solution.py
+++ b/solution.py
@@ -13,6 +13,7 @@
 
 NX, NY, NC = 4, 4, 2
 CHIPS = NX * NY
+OWN = CHIPS - 1
 PEERS = CHIPS * NC
 NZ = 8
 TOK = 128
@@ -24,6 +25,7 @@
 SHARD = D // NZ
 HALF = SHARD // 2
 PIECES = 7
+SLICES = 4
 
 
 def dot(a, b):
@@ -38,9 +40,12 @@
     return index // (NY * NC), lax.rem(index // NC, NY), lax.rem(index, NC)
 
 
+def far_first(v):
+    return 2 - v + 3 * (v // 2) - 2 * (v // 3)
+
+
 def offset(j, core):
-    p = lax.rem(j * 7, CHIPS)
-    a, b = p // NY, lax.rem(p, NY)
+    a, b = far_first(j // NY), far_first(lax.rem(j, NY))
     return a + core * (b - a), b + core * (a - b)
 
 
@@ -67,9 +72,9 @@
 
 
 def kernel(
-    ids_ref, prob_ref, tok_hbm, og_hbm, wg_hbm, wu_hbm, wd_hbm,
+    ids_hbm, prob_hbm, tok_hbm, og_hbm, wg_hbm, wu_hbm, wd_hbm,
     mixed_hbm, tgrad_hbm, gg_hbm, gu_hbm, gd_hbm,
-    tok, og, wg, wu, wd,
+    ids_ref, prob_ref, tok, og, wg, wu, wd,
     xs, ds, xr, dr, hid, dg, du, ca, cb,
     ov, dxv, orv, dxr,
     sp, sq, rp, rq, acc, mixed, tgrad, grads,
@@ -84,10 +89,13 @@
     loads = [
         pltpu.make_async_copy(src, dst, load_sem.at[i])
         for i, (src, dst) in enumerate(
-            [(tok_hbm, tok), (og_hbm, og), (wg_hbm.at[0], wg), (wu_hbm.at[0], wu), (wd_hbm.at[0], wd)]
+            [
+                (ids_hbm, ids_ref), (prob_hbm, prob_ref), (tok_hbm, tok), (og_hbm, og),
+                (wg_hbm.at[0], wg), (wu_hbm.at[0], wu), (wd_hbm.at[0], wd),
+            ]
         )
     ]
-    for load in loads:
+    for load in loads[:4]:
         load.start()
 
     barrier = pltpu.get_barrier_semaphore()
@@ -100,6 +108,9 @@
     loop(1, PEERS, greet)
     for other in (up, down):
         pl.semaphore_signal(barrier, inc=1, device_id={"dp": other}, device_id_type=MESH)
+
+    loads[0].wait()
+    loads[1].wait()
 
     sub = lax.broadcasted_iota(jnp.int32, (TOK, TOK), 0)
     lane = lax.broadcasted_iota(jnp.int32, (TOK, TOK), 1)
@@ -140,12 +151,14 @@
     def wide(n):
         return pl.ds(pl.multiple_of(n * WIDE, WIDE), WIDE)
 
-    loads[0].wait()
+    loads[2].wait()
 
     def build_x(n):
         xs[:, wide(n)] = dot(pick, tok[:, wide(n)]).astype(BF16)
 
     loop(0, D // WIDE, build_x)
+    for load in loads[4:]:
+        load.start()
     pl.semaphore_wait(barrier, PEERS - 1 + 2)
 
     def to_expert(src, dst, send_sem, recv_sem, j, t):
@@ -160,21 +173,23 @@
         )
 
     def own_block(src, dst, recv_sem):
-        return pltpu.make_async_copy(src.at[rows_of(me)], dst.at[rows_of(core)], recv_sem.at[core])
+        return pltpu.make_async_copy(
+            src.at[rows_of(me)], dst.at[rows_of(OWN * NC + core)], recv_sem.at[OWN * NC + core]
+        )
 
     def dispatch(src, dst, send_sem, recv_sem, t):
+        loop(0, OWN, lambda j: to_expert(src, dst, send_sem, recv_sem, j, t).start())
+
         @pl.when(core == t)
         def _():
             own_block(src, dst, recv_sem).start()
 
         @pl.when(core != t)
         def _():
-            to_expert(src, dst, send_sem, recv_sem, 0, t).start()
-
-        loop(1, CHIPS, lambda j: to_expert(src, dst, send_sem, recv_sem, j, t).start())
+            to_expert(src, dst, send_sem, recv_sem, OWN, t).start()
 
     dispatch(xs, xr, xss, xrs, 0)
-    loads[1].wait()
+    loads[3].wait()
 
     def build_dy(n):
         ds[:, wide(n)] = (dot(pick, og[:, wide(n)]) * slot_prob).astype(BF16)
@@ -193,8 +208,8 @@
     def tile(n):
         return pl.ds(pl.multiple_of(n * TILE, TILE), TILE)
 
-    loads[2].wait()
-    loads[3].wait()
+    loads[4].wait()
+    loads[5].wait()
 
     def forward(m):
         loop(0, MX // CAP, lambda i: arrived(xr, xrs, m * (MX // CAP) + i))
@@ -213,7 +228,7 @@
 
     loop(0, SLOTS // MX, forward)
 
-    loads[4].wait()
+    loads[6].wait()
     MD = 128
 
     def backward(m):
@@ -231,11 +246,13 @@
 
     right_sides = (dg, du, hid)
 
-    def left_sides(shard, half):
+    def part(shard, half, w, kept):
         cols = pl.ds(pl.multiple_of(shard * SHARD + half * HALF, HALF), HALF)
-        xt = jnp.transpose(xr[:, cols])
-        dt = jnp.transpose(dr[:, cols])
-        return xt, xt, dt
+        if w == 0:
+            kept[:] = [jnp.transpose(xr[:, cols])]
+        if w == 2:
+            kept[:] = [jnp.transpose(dr[:, cols])]
+        return dot(kept[0], right_sides[w][...])
 
     def shard_up(k):
         return lax.rem(z + 4 - (k + 1) // 2 + NZ, NZ), lax.rem(k + 1, 2)
@@ -262,10 +279,10 @@
     )
 
     def first(k):
-        lefts = [left_sides(*way[0](k)) for way in ways]
+        kept = [[], []]
         for w in range(3):
-            for left, (_, staged, got, send_sem, recv_sem, to) in zip(lefts, ways):
-                staged[k, third(w)] = dot(left[w], right_sides[w][...]).astype(BF16)
+            for left, (which, staged, got, send_sem, recv_sem, to) in zip(kept, ways):
+                staged[k, third(w)] = part(*which(k), w, left).astype(BF16)
                 pass_on(staged, k, got, send_sem, recv_sem, k, w, to).start()
 
     loop(0, 2, first)
@@ -283,11 +300,11 @@
         )
 
     def give_back(src, dst, send_sem, recv_sem, i):
-        @pl.when(i == core)
+        @pl.when(i == OWN * NC + core)
         def _():
             pltpu.make_async_copy(src.at[rows_of(i)], dst.at[rows_of(me)], recv_sem.at[me]).start()
 
-        @pl.when(i != core)
+        @pl.when(i != OWN * NC + core)
         def _():
             to_token(src, dst, send_sem, recv_sem, i).start()
 
@@ -309,12 +326,12 @@
         loop(0, MD // CAP, send)
 
     def later(k):
-        lefts = [left_sides(*way[0](k)) for way in ways]
+        kept = [[], []]
         for w in range(3):
-            for left, (_, staged, got, send_sem, recv_sem, to) in zip(lefts, ways):
-                part = dot(left[w], right_sides[w][...])
+            for left, (which, staged, got, send_sem, recv_sem, to) in zip(kept, ways):
+                mine = part(*which(k), w, left)
                 pass_on(got, k - 2, got, send_sem, recv_sem, k - 2, w, to).wait_recv()
-                got[k - 2, third(w)] = (part + got[k - 2, third(w)].astype(F32)).astype(BF16)
+                got[k - 2, third(w)] = (mine + got[k - 2, third(w)].astype(F32)).astype(BF16)
                 pass_on(got, k - 2, got, send_sem, recv_sem, k, w, to).start()
 
     def outputs_and_later(k):
@@ -346,9 +363,9 @@
         store.start()
 
     for half in range(2):
-        left = left_sides(z, half)
+        left = []
         for w in range(3):
-            acc[half, third(w)] = dot(left[w], right_sides[w][...])
+            acc[half, third(w)] = part(z, half, w, left)
     for w, out in enumerate((gg_hbm, gu_hbm, gd_hbm)):
         for k in (PIECES - 2, PIECES - 1):
             pass_on(rp, k, rp, pss, prs, k, w, up).wait_recv()
@@ -365,12 +382,12 @@
         to_expert(src, dst, send_sem, recv_sem, lax.rem(i, CHIPS), i // CHIPS).wait_send()
 
     def all_sent(i):
-        @pl.when(i != core * CHIPS)
+        @pl.when(i != core * CHIPS + OWN)
         def _():
             sent(xs, xr, xss, xrs, i)
             sent(ds, dr, dss, drs, i)
 
-        @pl.when(i != core)
+        @pl.when(i != OWN * NC + core)
         def _():
             to_token(ov, orv, oss, ors, i).wait_send()
             to_token(dxv, dxr, dxss, dxrs, i).wait_send()
@@ -389,10 +406,16 @@
 
 def hand_on(*refs):
     count = (len(refs) - 2) // 3
-    srcs, dsts, bufs = (refs[i * count : (i + 1) * count] for i in range(3))
+    arrays = [refs[i * count : (i + 1) * count] for i in range(3)]
     in_sem, out_sem = refs[3 * count :]
-    ins = [pltpu.make_async_copy(s, b, in_sem.at[i]) for i, (s, b) in enumerate(zip(srcs, bufs))]
-    outs = [pltpu.make_async_copy(b, d, out_sem.at[i]) for i, (b, d) in enumerate(zip(bufs, dsts))]
+    pieces = []
+    for array in zip(*arrays):
+        rows = array[0].shape[-2] // SLICES
+        for i in range(SLICES):
+            at = (0,) * (len(array[0].shape) - 2) + (pl.ds(i * rows, rows),)
+            pieces.append([ref.at[at] for ref in array])
+    ins = [pltpu.make_async_copy(s, b, in_sem.at[i]) for i, (s, d, b) in enumerate(pieces)]
+    outs = [pltpu.make_async_copy(b, d, out_sem.at[i]) for i, (s, d, b) in enumerate(pieces)]
     for copy in ins:
         copy.start()
     for copy, then in zip(ins, outs):
@@ -403,7 +426,6 @@
 
 
 def local(tokens, expert_ids, gate_probs, w_gate, w_up, w_down, out_grad):
-    vmem = pl.BlockSpec(memory_space=pltpu.VMEM)
     hbm = pl.BlockSpec(memory_space=pl.ANY)
     dma = pltpu.SemaphoreType.DMA
     slots = lambda: pltpu.VMEM((SLOTS, D), BF16)
@@ -418,9 +440,11 @@
     results = pl.pallas_call(
         kernel,
         out_shape=shapes,
-        in_specs=[vmem, vmem] + [hbm] * 5,
+        in_specs=[hbm] * 7,
         out_specs=(hbm,) * 5,
         scratch_shapes=[
+            pltpu.VMEM((TOP, TOK), jnp.int32),
+            pltpu.VMEM((TOP, TOK), F32),
             pltpu.VMEM((TOK, D), BF16),
             pltpu.VMEM((TOK, D), BF16),
             pltpu.VMEM((D, H), BF16),
@@ -437,7 +461,7 @@
             pltpu.VMEM((TOK, D), BF16),
             pltpu.VMEM((TOK, D), BF16),
             pltpu.VMEM((3, SHARD, H), BF16),
-            dma((5,)), dma((5,)),
+            dma((7,)), dma((5,)),
             dma((PEERS,)), dma((PEERS,)), dma((PEERS,)), dma((PEERS,)),
             dma((PEERS,)), dma((PEERS,)), dma((PEERS,)), dma((PEERS,)),
             dma((PIECES * 3,)), dma((PIECES * 3,)), dma((PIECES * 3,)), dma((PIECES * 3,)),
@@ -452,7 +476,8 @@
         out_shape=shapes,
         in_specs=[hbm] * 5,
         out_specs=(hbm,) * 5,
-        scratch_shapes=[pltpu.VMEM(shape.shape, shape.dtype) for shape in shapes] + [dma((5,)), dma((5,))],
+        scratch_shapes=[pltpu.VMEM(shape.shape, shape.dtype) for shape in shapes]
+        + [dma((5 * SLICES,)), dma((5 * SLICES,))],
         name="hand_on",
     )(*results)
 

time: 138 us -> 141 us (1.022)
  Pallas kernels: 137 us -> 140 us
    pallas_call x1, Pallas kernels: 135 us -> 137 us  [local(): pl.pallas_call(kernel, out_shape=shapes, in_specs=[hbm] * 7, out_specs=(h...]
where the time goes in v3:
time: 141 us; the launch traced here: 140 us
  Pallas kernels  140 us (99%)
    pallas_call x1, Pallas kernels, local(): pl.pallas_call(kernel, out_shape=shapes, in_specs=[hbm] * 7, out_specs=(h...  137 us

profile of v3, /device:TPU:1, one launch (start us, length us, event | category | flops | bytes accessed | tf_op | source)
XLA Modules:
  0.0 140.4 jit_solution(11294793993065785216)
XLA Ops:
  0.6 137.0 %expert_layer.1 = (bf16[128,2048]{1,0:T(8,128)(2,1)}, bf16[128,2048]{1,0:T(8,128)(2,1)}, bf16[1,256,768]{2,1,0:T(8,128)(2,1)}, bf16[1,256,768]{2,1,0:T(8,128)(2,1)}, bf16[1,256,768]{2,1,0:T(8,128)(2,1)}) custom-call(s32[2,128]{1,0:T(2,128)} %bitcast.2, f32[2,128]{1,0:T(2,128)} %bitcast.3, bf16[128,2048]{1,0:T(8,128)(2,1)} %tok_hbm.1, ...), custom_call_target="tpu_custom_call" | custom-call | tf_op jit(solution)/shard_map/expert_layer/pallas_call | solution.py:440
  137.7 2.7 %hand_on.1 = (bf16[128,2048]{1,0:T(8,128)(2,1)}, bf16[128,2048]{1,0:T(8,128)(2,1)}, bf16[1,256,768]{2,1,0:T(8,128)(2,1)}, bf16[1,256,768]{2,1,0:T(8,128)(2,1)}, bf16[1,256,768]{2,1,0:T(8,128)(2,1)}) custom-call(bf16[128,2048]{1,0:T(8,128)(2,1)} %get-tuple-element.10.refs_0_, bf16[128,2048]{1,0:T(8,128)(2,1)} %get-tuple-element.11.refs_1_, ...), custom_call_target="tpu_custom_call" | custom-call | tf_op jit(solution)/shard_map/hand_on/pallas_call | solution.py:474

commit v4 on v3

--- a/solution.py
+++ b/solution.py
@@ -25,7 +25,6 @@
 SHARD = D // NZ
 HALF = SHARD // 2
 PIECES = 7
-SLICES = 4
 
 
 def dot(a, b):
@@ -40,12 +39,9 @@
     return index // (NY * NC), lax.rem(index // NC, NY), lax.rem(index, NC)
 
 
-def far_first(v):
-    return 2 - v + 3 * (v // 2) - 2 * (v // 3)
-
-
 def offset(j, core):
-    a, b = far_first(j // NY), far_first(lax.rem(j, NY))
+    p = lax.rem((j + 1) * 7, CHIPS)
+    a, b = p // NY, lax.rem(p, NY)
     return a + core * (b - a), b + core * (a - b)
 
 
@@ -78,7 +74,7 @@
     xs, ds, xr, dr, hid, dg, du, ca, cb,
     ov, dxv, orv, dxr,
     sp, sq, rp, rq, acc, mixed, tgrad, grads,
-    load_sem, store_sem, xss, dss, oss, dxss, xrs, drs, ors, dxrs, pss, qss, prs, qrs,
+    load_sem, store_sem, xss, dss, oss, dxss, xrs, drs, ors, dxrs, pss, qss, prs, qrs, turn,
 ):
     me = lax.axis_index("expert")
     z = lax.axis_index("dp")
@@ -196,8 +192,15 @@
 
     loop(0, D // WIDE, build_dy)
     dispatch(ds, dr, dss, drs, 0)
-    dispatch(xs, xr, xss, xrs, 1)
-    dispatch(ds, dr, dss, drs, 1)
+
+    def dispatch_second():
+        dispatch(xs, xr, xss, xrs, 1)
+        dispatch(ds, dr, dss, drs, 1)
+
+    @pl.when(core == 1)
+    def _():
+        pl.semaphore_wait(turn, 1)
+        dispatch_second()
 
     def arrived(dst, recv_sem, i):
         pltpu.make_async_copy(dst.at[rows_of(i)], dst.at[rows_of(i)], recv_sem.at[i]).wait()
@@ -243,6 +246,10 @@
         loop(0, H // TILE, columns)
 
     loop(0, SLOTS // MD, backward)
+
+    @pl.when(core == 0)
+    def _():
+        pl.semaphore_signal(turn, inc=1, device_id={"expert": me + 1}, device_id_type=MESH)
 
     right_sides = (dg, du, hid)
 
@@ -286,6 +293,10 @@
                 pass_on(staged, k, got, send_sem, recv_sem, k, w, to).start()
 
     loop(0, 2, first)
+
+    @pl.when(core == 0)
+    def _():
+        dispatch_second()
 
     def to_token(src, dst, send_sem, recv_sem, i):
         j, c = i // NC, lax.rem(i, NC)
@@ -406,16 +417,10 @@
 
 def hand_on(*refs):
     count = (len(refs) - 2) // 3
-    arrays = [refs[i * count : (i + 1) * count] for i in range(3)]
+    srcs, dsts, bufs = (refs[i * count : (i + 1) * count] for i in range(3))
     in_sem, out_sem = refs[3 * count :]
-    pieces = []
-    for array in zip(*arrays):
-        rows = array[0].shape[-2] // SLICES
-        for i in range(SLICES):
-            at = (0,) * (len(array[0].shape) - 2) + (pl.ds(i * rows, rows),)
-            pieces.append([ref.at[at] for ref in array])
-    ins = [pltpu.make_async_copy(s, b, in_sem.at[i]) for i, (s, d, b) in enumerate(pieces)]
-    outs = [pltpu.make_async_copy(b, d, out_sem.at[i]) for i, (s, d, b) in enumerate(pieces)]
+    ins = [pltpu.make_async_copy(s, b, in_sem.at[i]) for i, (s, b) in enumerate(zip(srcs, bufs))]
+    outs = [pltpu.make_async_copy(b, d, out_sem.at[i]) for i, (b, d) in enumerate(zip(bufs, dsts))]
     for copy in ins:
         copy.start()
     for copy, then in zip(ins, outs):
@@ -465,6 +470,7 @@
             dma((PEERS,)), dma((PEERS,)), dma((PEERS,)), dma((PEERS,)),
             dma((PEERS,)), dma((PEERS,)), dma((PEERS,)), dma((PEERS,)),
             dma((PIECES * 3,)), dma((PIECES * 3,)), dma((PIECES * 3,)), dma((PIECES * 3,)),
+            pltpu.SemaphoreType.REGULAR,
         ],
         compiler_params=pltpu.CompilerParams(
             collective_id=0, has_side_effects=True, vmem_limit_bytes=62 * 2**20
@@ -476,8 +482,7 @@
         out_shape=shapes,
         in_specs=[hbm] * 5,
         out_specs=(hbm,) * 5,
-        scratch_shapes=[pltpu.VMEM(shape.shape, shape.dtype) for shape in shapes]
-        + [dma((5 * SLICES,)), dma((5 * SLICES,))],
+        scratch_shapes=[pltpu.VMEM(shape.shape, shape.dtype) for shape in shapes] + [dma((5,)), dma((5,))],
         name="hand_on",
     )(*results)
 

time: 141 us -> 137 us (0.972)
  Pallas kernels: 140 us -> 136 us
    pallas_call x1, Pallas kernels: 137 us -> 133 us  [local(): pl.pallas_call(kernel, out_shape=shapes, in_specs=[hbm] * 7, out_specs=(h...]
where the time goes in v4:
time: 137 us
  Pallas kernels  136 us (99%)
    pallas_call x1, Pallas kernels, local(): pl.pallas_call(kernel, out_shape=shapes, in_specs=[hbm] * 7, out_specs=(h...  133 us

profile of v4, /device:TPU:1, one launch (start us, length us, event | category | flops | bytes accessed | tf_op | source)
XLA Modules:
  0.0 136.6 jit_solution(7934147176667647061)
XLA Ops:
  0.6 133.5 %expert_layer.1 = (bf16[128,2048]{1,0:T(8,128)(2,1)}, bf16[128,2048]{1,0:T(8,128)(2,1)}, bf16[1,256,768]{2,1,0:T(8,128)(2,1)}, bf16[1,256,768]{2,1,0:T(8,128)(2,1)}, bf16[1,256,768]{2,1,0:T(8,128)(2,1)}) custom-call(s32[2,128]{1,0:T(2,128)} %bitcast.2, f32[2,128]{1,0:T(2,128)} %bitcast.3, bf16[128,2048]{1,0:T(8,128)(2,1)} %tok_hbm.1, ...), custom_call_target="tpu_custom_call" | custom-call | tf_op jit(solution)/shard_map/expert_layer/pallas_call | solution.py:445
  134.1 2.5 %hand_on.1 = (bf16[128,2048]{1,0:T(8,128)(2,1)}, bf16[128,2048]{1,0:T(8,128)(2,1)}, bf16[1,256,768]{2,1,0:T(8,128)(2,1)}, bf16[1,256,768]{2,1,0:T(8,128)(2,1)}, bf16[1,256,768]{2,1,0:T(8,128)(2,1)}) custom-call(bf16[128,2048]{1,0:T(8,128)(2,1)} %get-tuple-element.10.refs_0_, bf16[128,2048]{1,0:T(8,128)(2,1)} %get-tuple-element.11.refs_1_, ...), custom_call_target="tpu_custom_call" | custom-call | tf_op jit(solution)/shard_map/hand_on/pallas_call | solution.py:480

commit v5 on v4

--- a/solution.py
+++ b/solution.py
@@ -40,7 +40,7 @@
 
 
 def offset(j, core):
-    p = lax.rem((j + 1) * 7, CHIPS)
+    p = lax.rem((j + 1) * 5, CHIPS)
     a, b = p // NY, lax.rem(p, NY)
     return a + core * (b - a), b + core * (a - b)
 
@@ -133,7 +133,9 @@
     slot_row = [to_row(slot_col[k]) for k in range(TOP)]
     prob_row = [probs[k : k + 1] for k in range(TOP)]
     prob_col = [to_col(prob_row[k]) for k in range(TOP)]
-    slot_of = lax.broadcasted_iota(jnp.int32, (SLOTS, TOK), 0).astype(F32)
+    row = lax.broadcasted_iota(jnp.int32, (SLOTS, TOK), 0)
+    block = row // CAP
+    slot_of = (((block % CHIPS) * NC + block // CHIPS) * CAP + row % CAP).astype(F32)
     owner = [slot_of == slot_row[k] for k in range(TOP)]
     pick = jnp.where(owner[0] | owner[1], 1.0, 0.0).astype(BF16)
     slot_prob = jnp.sum(
@@ -149,10 +151,25 @@
 
     loads[2].wait()
 
-    def build_x(n):
-        xs[:, wide(n)] = dot(pick, tok[:, wide(n)]).astype(BF16)
-
-    loop(0, D // WIDE, build_x)
+    CORE_ROWS = SLOTS // NC
+
+    def build_x(t):
+        rows = slice(t * CORE_ROWS, (t + 1) * CORE_ROWS)
+
+        def columns(n):
+            xs[rows, wide(n)] = dot(pick[rows], tok[:, wide(n)]).astype(BF16)
+
+        loop(0, D // WIDE, columns)
+
+    def build_dy(t):
+        rows = slice(t * CORE_ROWS, (t + 1) * CORE_ROWS)
+
+        def columns(n):
+            ds[rows, wide(n)] = (dot(pick[rows], og[:, wide(n)]) * slot_prob[rows]).astype(BF16)
+
+        loop(0, D // WIDE, columns)
+
+    build_x(0)
     for load in loads[4:]:
         load.start()
     pl.semaphore_wait(barrier, PEERS - 1 + 2)
@@ -160,7 +177,7 @@
     def to_expert(src, dst, send_sem, recv_sem, j, t):
         peer = ahead(x, y, core, t, j)
         return pltpu.make_async_remote_copy(
-            src.at[rows_of(peer)],
+            src.at[rows_of(t * CHIPS + peer // NC)],
             dst.at[rows_of(j * NC + core)],
             send_sem.at[t * CHIPS + j],
             recv_sem.at[j * NC + core],
@@ -170,7 +187,7 @@
 
     def own_block(src, dst, recv_sem):
         return pltpu.make_async_copy(
-            src.at[rows_of(me)], dst.at[rows_of(OWN * NC + core)], recv_sem.at[OWN * NC + core]
+            src.at[rows_of(core * CHIPS + me // NC)], dst.at[rows_of(OWN * NC + core)], recv_sem.at[OWN * NC + core]
         )
 
     def dispatch(src, dst, send_sem, recv_sem, t):
@@ -187,11 +204,10 @@
     dispatch(xs, xr, xss, xrs, 0)
     loads[3].wait()
 
-    def build_dy(n):
-        ds[:, wide(n)] = (dot(pick, og[:, wide(n)]) * slot_prob).astype(BF16)
-
-    loop(0, D // WIDE, build_dy)
+    build_dy(0)
     dispatch(ds, dr, dss, drs, 0)
+    build_x(1)
+    build_dy(1)
 
     def dispatch_second():
         dispatch(xs, xr, xss, xrs, 1)

time: 137 us -> 136 us (level)
  no operation moved by 1% of the time
where the time goes in v5:
time: 136 us
  Pallas kernels  136 us (100%)
    pallas_call x1, Pallas kernels, local(): pl.pallas_call(kernel, out_shape=shapes, in_specs=[hbm] * 7, out_specs=(h...  133 us

profile of v5, /device:TPU:1, one launch (start us, length us, event | category | flops | bytes accessed | tf_op | source)
XLA Modules:
  0.0 136.3 jit_solution(3302890614066979403)
XLA Ops:
  0.6 133.2 %expert_layer.1 = (bf16[128,2048]{1,0:T(8,128)(2,1)}, bf16[128,2048]{1,0:T(8,128)(2,1)}, bf16[1,256,768]{2,1,0:T(8,128)(2,1)}, bf16[1,256,768]{2,1,0:T(8,128)(2,1)}, bf16[1,256,768]{2,1,0:T(8,128)(2,1)}) custom-call(s32[2,128]{1,0:T(2,128)} %bitcast.2, f32[2,128]{1,0:T(2,128)} %bitcast.3, bf16[128,2048]{1,0:T(8,128)(2,1)} %tok_hbm.1, ...), custom_call_target="tpu_custom_call" | custom-call | tf_op jit(solution)/shard_map/expert_layer/pallas_call | solution.py:461
  133.8 2.5 %hand_on.1 = (bf16[128,2048]{1,0:T(8,128)(2,1)}, bf16[128,2048]{1,0:T(8,128)(2,1)}, bf16[1,256,768]{2,1,0:T(8,128)(2,1)}, bf16[1,256,768]{2,1,0:T(8,128)(2,1)}, bf16[1,256,768]{2,1,0:T(8,128)(2,1)}) custom-call(bf16[128,2048]{1,0:T(8,128)(2,1)} %get-tuple-element.10.refs_0_, bf16[128,2048]{1,0:T(8,128)(2,1)} %get-tuple-element.11.refs_1_, ...), custom_call_target="tpu_custom_call" | custom-call | tf_op jit(solution)/shard_map/hand_on/pallas_call | solution.py:496
